TPU v7x, 128 devices: a whole 4x4x4 slice. The times are simulated.
128 devices in a mesh: dp: 2 (over core), lat: 8 (over z, y_hi), lon: 8 (over y_lo, x).
Axes of the slice: x: 4, y: 4 (y_hi: 2, y_lo: 2; y = y_hi * 2 + y_lo), z: 4, core: 2. Of those that a mesh axis runs over, the one named last changes fastest.
Arguments:
- fields: bfloat16 [2, 640, 1024, 128], P('dp', 'lat', 'lon'), may hold values from -6 to 6
- down_weight: bfloat16 [3, 3, 128, 128], P(None, None, 'dp'), may hold values from -0.1875 to 0.1875
- mid_weight: bfloat16 [3, 3, 128, 128], P(None, None, 'dp'), may hold values from -0.1875 to 0.1875
- up_weight: bfloat16 [3, 3, 128, 128], P(None, None, 'dp'), may hold values from -0.1875 to 0.1875
- cotangent: bfloat16 [2, 640, 1024, 128], P('dp', 'lat', 'lon'), may hold values from -6 to 6
Outputs:
- level_out: bfloat16 [2, 640, 1024, 128], P('dp', 'lat', 'lon')
- grad_fields: bfloat16 [2, 640, 1024, 128], P('dp', 'lat', 'lon')
- grad_down: float32 [3, 3, 128, 128], P(None, None, 'dp')
- grad_mid: float32 [3, 3, 128, 128], P(None, None, 'dp')
- grad_up: float32 [3, 3, 128, 128], P(None, None, 'dp')
All inputs are finite; a program needn't handle non-finite values.
Results may differ from a plain program's by a relative error of at most 0.012.
Values may be sent and summed in bfloat16 or wider, within the bound.
No kernel may reach another device: no remote copies, remote signals or barrier semaphores. Data moves between devices by JAX's collectives and lax.ppermute only.
A program may use at most 128 MiB of HBM per device.

v0:
```python
import math
import jax
import jax.numpy as jnp
from jax import lax
from jax.sharding import PartitionSpec as P


def extended(block, sides, width, periodic):
    for axis, dim in sides:
        count = lax.axis_size(axis)
        forward = [(i, i + 1) for i in range(count - 1)]
        if periodic:
            forward.append((count - 1, 0))
        backward = [(target, source) for source, target in forward]
        low = lax.ppermute(
            lax.slice_in_dim(block, block.shape[dim] - width, None, axis=dim), axis, forward
        )
        high = lax.ppermute(lax.slice_in_dim(block, 0, width, axis=dim), axis, backward)
        block = jnp.concatenate([low, block, high], axis=dim)
    return block


def framed(field):
    tall = extended(field, (("lat", 1),), 1, False)
    return extended(tall, (("lon", 2),), 1, True)


def convolve(padded, kernel, stride, dilate, padding):
    return lax.conv_general_dilated(
        padded,
        kernel,
        (stride, stride),
        padding,
        lhs_dilation=(dilate, dilate),
        dimension_numbers=("NHWC", "HWIO", "NHWC"),
        preferred_element_type=jnp.float32,
    )


def taps_down(padded, kernel):
    return convolve(padded, kernel, 2, 1, "VALID")


def taps_same(padded, kernel):
    return convolve(padded, kernel, 1, 1, "VALID")


def taps_up(padded, kernel):
    return convolve(padded, kernel[::-1, ::-1], 1, 2, ((-1, 0), (-1, 0)))


def kernel_grad(padded, grad, dilate, layout):
    result = lax.conv_general_dilated(
        padded,
        grad,
        (1, 1),
        "VALID",
        rhs_dilation=(dilate, dilate),
        dimension_numbers=("CHWN", "IHWO", layout),
        preferred_element_type=jnp.float32,
    )
    return result[:3, :3]


def swap_io(kernel):
    return jnp.transpose(kernel, (0, 1, 3, 2))


def body(fields, down_weight, mid_weight, up_weight, cotangent):
    kernel_down, kernel_mid, kernel_up = (
        lax.all_gather(down_weight, "dp", axis=2, tiled=True),
        lax.all_gather(mid_weight, "dp", axis=2, tiled=True),
        lax.all_gather(up_weight, "dp", axis=2, tiled=True),
    )
    cells = (
        fields.shape[0]
        * lax.axis_size("dp")
        * fields.shape[1]
        * lax.axis_size("lat")
        * fields.shape[2]
        * lax.axis_size("lon")
    )
    scale = 1.0 / math.sqrt(cells)
    framed_in = framed(fields)
    down = taps_down(framed_in, kernel_down).astype(jnp.bfloat16)
    framed_down = framed(down)
    pre = taps_same(framed_down, kernel_mid)
    mid = jax.nn.silu(pre).astype(jnp.bfloat16)
    framed_mid = framed(mid)
    level_out = (fields.astype(jnp.float32) + taps_up(framed_mid, kernel_up)).astype(jnp.bfloat16)
    framed_cot = framed(cotangent)
    up_term = kernel_grad(framed_cot, mid, 2, "HWCN") * scale
    grad_mid_map = taps_down(framed_cot, swap_io(kernel_up))
    sig = jax.nn.sigmoid(pre)
    grad_pre = (grad_mid_map * sig * (1.0 + pre * (1.0 - sig))).astype(jnp.bfloat16)
    mid_term = kernel_grad(framed_down, grad_pre, 1, "HWNC") * scale
    grad_down_map = taps_same(framed(grad_pre), swap_io(kernel_mid)[::-1, ::-1]).astype(
        jnp.bfloat16
    )
    down_term = kernel_grad(framed_in, grad_down_map, 2, "HWNC") * scale
    grad_fields = (
        cotangent.astype(jnp.float32) + taps_up(framed(grad_down_map), swap_io(kernel_down))
    ).astype(jnp.bfloat16)
    totals = lax.psum((down_term, mid_term, up_term), ("lat", "lon"))
    grad_down, grad_mid, grad_up = (
        lax.psum_scatter(
            totals[0].astype(jnp.bfloat16), "dp", scatter_dimension=2, tiled=True
        ).astype(jnp.float32),
        lax.psum_scatter(
            totals[1].astype(jnp.bfloat16), "dp", scatter_dimension=2, tiled=True
        ).astype(jnp.float32),
        lax.psum_scatter(
            totals[2].astype(jnp.bfloat16), "dp", scatter_dimension=2, tiled=True
        ).astype(jnp.float32),
    )
    return (level_out, grad_fields, grad_down, grad_mid, grad_up)


def solution(mesh):
    in_specs = (
        P("dp", "lat", "lon", None),
        P(None, None, "dp", None),
        P(None, None, "dp", None),
        P(None, None, "dp", None),
        P("dp", "lat", "lon", None),
    )
    out_specs = (
        P("dp", "lat", "lon", None),
        P("dp", "lat", "lon", None),
        P(None, None, "dp", None),
        P(None, None, "dp", None),
        P(None, None, "dp", None),
    )
    return jax.shard_map(body, mesh=mesh, in_specs=in_specs, out_specs=out_specs, check_vma=False)
```

profile of v0, /device:TPU:16, one launch (start us, length us, event | category | flops | bytes accessed | tf_op | source)
XLA Modules:
  0.0 591.8 jit_solution(1721154471314080505)
XLA Ops:
  10.2 6.1 %collective-permute-start = (bf16[1,1,128,128]{3,2,1,0:T(8,128)(2,1)S(1)}, bf16[1,1,128,128]{3,2,1,0:T(8,128)(2,1)S(1)}, u32[]{:S(2)}, u32[]{:S(2)}) collective-permute-start(bf16[1,1,128,128]{3,2,1,0:T(8,128)(2,1)S(1)} %get-tuple-element.33), channel_id=1, source_target_pairs={{0,8},{8,16},{16,24},{24,32},{32,40},{40,48},{48,56},{1,9},{9,17},... | collective-permute-start | bytes 98312 | tf_op jit(solution)/shard_map/ppermute | solution.py:15
  18.9 6.3 %collective-permute-start.12 = (bf16[1,1,128,128]{3,2,1,0:T(8,128)(2,1)S(1)}, bf16[1,1,128,128]{3,2,1,0:T(8,128)(2,1)S(1)}, u32[]{:S(2)}, u32[]{:S(2)}) collective-permute-start(bf16[1,1,128,128]{3,2,1,0:T(8,128)(2,1)S(1)} %get-tuple-element.31), channel_id=1, source_target_pairs={{0,8},{8,16},{16,24},{24,32},{32,40},{40,48},{48,56},{1,9},{9,17},... | collective-permute-start | bytes 98312 | tf_op jit(solution)/shard_map/ppermute | solution.py:15
  27.6 3.7 all_gather.10
  31.3 3.9 all_gather.11
  39.6 2.6 collective-permute-start.3
  42.4 4.6 collective-permute-start.15
  63.9 5.1 collective-permute-start.5
  69.1 4.4 fusion.132
  80.8 4.1 collective-permute-start.7
  103.5 3.3 collective-permute-start.8
  106.8 4.6 collective-permute-start.9
  114.1 3.6 collective-permute-start.16
  117.8 4.1 collective-permute-start.17
  123.1 5.3 fusion.79
  131.0 4.1 collective-permute-start.19
  140.6 3.6 fusion.76
  144.2 346.6 %all-reduce.2 = (bf16[3,3,128,128]{3,2,1,0:T(8,128)(2,1)}, bf16[3,3,128,128]{3,2,1,0:T(8,128)(2,1)}, bf16[3,3,128,128]{3,2,1,0:T(8,128)(2,1)}) all-reduce(f32[3,3,128,128]{3,2,1,0:T(8,128)} %fusion.76, f32[3,3,128,128]{3,2,1,0:T(8,128)S(1)} %copy-done.25, ...), channel_id=1, replica_groups=mesh['dp'=2,'lat'=8,'lon'=8] {'lat','lon'}, use_global_device_ids=true, to_apply=%region_0.1 | all-reduce | flops 442368 | bytes 2654208 | tf_op jit(solution)/shard_map/psum | solution.py:104
  492.8 4.1 collective-permute-start.11
  500.2 22.3 %collective-permute-start.21 = (bf16[1,1,64,128]{3,0,2,1:T(2,128)(2,1)S(1)}, bf16[1,1,64,128]{3,0,2,1:T(2,128)(2,1)S(1)}, u32[]{:S(2)}, u32[]{:S(2)}) collective-permute-start(bf16[1,1,64,128]{3,0,2,1:T(2,128)(2,1)S(1)} %slice.175), channel_id=1, source_target_pairs={{8,0},{16,8},{24,16},{32,24},{40,32},{48,40},{56,48},{9,1},{17,9},... | collective-permute-start | bytes 49160 | tf_op jit(solution)/shard_map/ppermute | solution.py:18
  522.7 3.7 pad_maximum_fusion.15
  529.1 3.2 collective-permute-start.23
  532.3 20.0 %fusion.21 = bf16[1,80,128,128]{3,0,2,1:T(2,128)(2,1)S(1)} fusion(bf16[1,80,128,128]{3,2,1,0:T(8,128)(2,1)S(1)} %copy-done.12, bf16[3,3,128,128]{3,2,1,0:T(8,128)(2,1)S(1)} %copy-done.29, bf16[1,42,66,128]{3,0,2,1:T(2,128)(2,1)S(1)} %pad_maximum_fusion.15), kind=kOutput, calls=%fused_computation.25 | convolution fusion | flops 758906880 | bytes 6247424 | tf_op jit(solution)/shard_map/conv_general_dilated | solution.py:29
  554.4 3.7 pad_maximum_fusion.14
  558.1 20.0 %fusion.19 = bf16[1,80,128,128]{3,0,2,1:T(2,128)(2,1)S(1)} fusion(bf16[1,80,128,128]{3,2,1,0:T(8,128)(2,1)S(1)} %copy-done.14, bf16[3,3,128,128]{3,2,1,0:T(8,128)(2,1)S(1)} %copy-done.27, bf16[1,42,66,128]{3,0,2,1:T(2,128)(2,1)S(1)} %pad_maximum_fusion.14), kind=kOutput, calls=%fused_computation.22 | convolution fusion | flops 758906880 | bytes 6247424 | tf_op jit(solution)/shard_map/conv_general_dilated | solution.py:29
  (213 shorter events, 83.6 us)
Async XLA Ops:
  7.2 572.9 %reduce-scatter.8.cloned.1.call-start = ((), (), s32[]{:S(2)}) async-start(), calls=%async_computation.5 | async-start | bytes 442368 | tf_op jit(solution)/shard_map/reduce_scatter | solution.py:112
  8.0 29.6 %collective-permute-start.1 = (bf16[1,1,128,128]{3,2,1,0:T(8,128)(2,1)S(1)}, bf16[1,1,128,128]{3,2,1,0:T(8,128)(2,1)S(1)}, u32[]{:S(2)}, u32[]{:S(2)}) collective-permute-start(bf16[1,1,128,128]{3,2,1,0:T(8,128)(2,1)S(1)} %get-tuple-element.32), channel_id=1, source_target_pairs={{8,0},{16,8},{24,16},{32,24},{40,32},{48,40},{56,48},{9,1},{17,9},... | collective-permute-start | bytes 98312 | tf_op jit(solution)/shard_map/ppermute | solution.py:18
  10.2 25.0 %collective-permute-start = (bf16[1,1,128,128]{3,2,1,0:T(8,128)(2,1)S(1)}, bf16[1,1,128,128]{3,2,1,0:T(8,128)(2,1)S(1)}, u32[]{:S(2)}, u32[]{:S(2)}) collective-permute-start(bf16[1,1,128,128]{3,2,1,0:T(8,128)(2,1)S(1)} %get-tuple-element.33), channel_id=1, source_target_pairs={{0,8},{8,16},{16,24},{24,32},{32,40},{40,48},{48,56},{1,9},{9,17},... | collective-permute-start | bytes 98312 | tf_op jit(solution)/shard_map/ppermute | solution.py:15
  17.0 25.2 %collective-permute-start.13 = (bf16[1,1,128,128]{3,2,1,0:T(8,128)(2,1)S(1)}, bf16[1,1,128,128]{3,2,1,0:T(8,128)(2,1)S(1)}, u32[]{:S(2)}, u32[]{:S(2)}) collective-permute-start(bf16[1,1,128,128]{3,2,1,0:T(8,128)(2,1)S(1)} %get-tuple-element.30), channel_id=1, source_target_pairs={{8,0},{16,8},{24,16},{32,24},{40,32},{48,40},{56,48},{9,1},{17,9},... | collective-permute-start | bytes 98312 | tf_op jit(solution)/shard_map/ppermute | solution.py:18
  18.9 18.7 %collective-permute-start.12 = (bf16[1,1,128,128]{3,2,1,0:T(8,128)(2,1)S(1)}, bf16[1,1,128,128]{3,2,1,0:T(8,128)(2,1)S(1)}, u32[]{:S(2)}, u32[]{:S(2)}) collective-permute-start(bf16[1,1,128,128]{3,2,1,0:T(8,128)(2,1)S(1)} %get-tuple-element.31), channel_id=1, source_target_pairs={{0,8},{8,16},{16,24},{24,32},{32,40},{40,48},{48,56},{1,9},{9,17},... | collective-permute-start | bytes 98312 | tf_op jit(solution)/shard_map/ppermute | solution.py:15
  38.0 8.9 %collective-permute-start.2 = (bf16[1,82,1,128]{3,2,1,0:T(2,128)(2,1)S(1)}, bf16[1,82,1,128]{3,2,1,0:T(2,128)(2,1)S(1)}, u32[]{:S(2)}, u32[]{:S(2)}) collective-permute-start(bf16[1,82,1,128]{3,2,1,0:T(2,128)(2,1)S(1)} %get-tuple-element.28), channel_id=1, source_target_pairs={{0,1},{1,2},{2,3},{3,4},{4,5},{5,6},{6,7},{7,0},{8,9},{9,10},{10,1... | collective-permute-start | bytes 62984 | tf_op jit(solution)/shard_map/ppermute | solution.py:15
  42.3 11.2 %collective-permute-start.14 = (bf16[1,82,1,128]{3,2,1,0:T(2,128)(2,1)S(1)}, bf16[1,82,1,128]{3,2,1,0:T(2,128)(2,1)S(1)}, u32[]{:S(2)}, u32[]{:S(2)}) collective-permute-start(bf16[1,82,1,128]{3,2,1,0:T(2,128)(2,1)S(1)} %get-tuple-element.26), channel_id=1, source_target_pairs={{0,1},{1,2},{2,3},{3,4},{4,5},{5,6},{6,7},{7,0},{8,9},{9,10},{10,1... | collective-permute-start | bytes 62984 | tf_op jit(solution)/shard_map/ppermute | solution.py:15
  42.4 11.1 %collective-permute-start.15 = (bf16[1,82,1,128]{3,2,1,0:T(2,128)(2,1)S(1)}, bf16[1,82,1,128]{3,2,1,0:T(2,128)(2,1)S(1)}, u32[]{:S(2)}, u32[]{:S(2)}) collective-permute-start(bf16[1,82,1,128]{3,2,1,0:T(2,128)(2,1)S(1)} %get-tuple-element.27), channel_id=1, source_target_pairs={{1,0},{2,1},{3,2},{4,3},{5,4},{6,5},{7,6},{0,7},{9,8},{10,9},{11,1... | collective-permute-start | bytes 62984 | tf_op jit(solution)/shard_map/ppermute | solution.py:18
  61.5 18.3 %collective-permute-start.4 = (bf16[1,1,64,128]{3,2,1,0:T(8,128)(2,1)S(1)}, bf16[1,1,64,128]{3,2,1,0:T(8,128)(2,1)S(1)}, u32[]{:S(2)}, u32[]{:S(2)}) collective-permute-start(bf16[1,1,64,128]{3,2,1,0:T(8,128)(2,1)S(1)} %slice.150), channel_id=1, source_target_pairs={{0,8},{8,16},{16,24},{24,32},{32,40},{40,48},{48,56},{1,9},{9,17},... | collective-permute-start | bytes 49160 | tf_op jit(solution)/shard_map/ppermute | solution.py:15
  63.9 15.9 %collective-permute-start.5 = (bf16[1,1,64,128]{3,1,2,0:T(2,128)(2,1)S(1)}, bf16[1,1,64,128]{3,1,2,0:T(2,128)(2,1)S(1)}, u32[]{:S(2)}, u32[]{:S(2)}) collective-permute-start(bf16[1,1,64,128]{3,1,2,0:T(2,128)(2,1)S(1)} %slice.153), channel_id=1, source_target_pairs={{8,0},{16,8},{24,16},{32,24},{40,32},{48,40},{56,48},{9,1},{17,9},... | collective-permute-start | bytes 49160 | tf_op jit(solution)/shard_map/ppermute | solution.py:18
  80.7 10.4 %collective-permute-start.6 = (bf16[1,42,1,128]{3,1,2,0:T(8,128)(2,1)S(1)}, bf16[1,42,1,128]{3,1,2,0:T(8,128)(2,1)S(1)}, u32[]{:S(2)}, u32[]{:S(2)}) collective-permute-start(bf16[1,42,1,128]{3,1,2,0:T(8,128)(2,1)S(1)} %get-tuple-element.52), channel_id=1, source_target_pairs={{0,1},{1,2},{2,3},{3,4},{4,5},{5,6},{6,7},{7,0},{8,9},{9,10},{10,1... | collective-permute-start | bytes 32264 | tf_op jit(solution)/shard_map/ppermute | solution.py:15
  80.8 10.3 %collective-permute-start.7 = (bf16[1,42,1,128]{3,1,2,0:T(8,128)(2,1)S(1)}, bf16[1,42,1,128]{3,1,2,0:T(8,128)(2,1)S(1)}, u32[]{:S(2)}, u32[]{:S(2)}) collective-permute-start(bf16[1,42,1,128]{3,1,2,0:T(8,128)(2,1)S(1)} %get-tuple-element.53), channel_id=1, source_target_pairs={{1,0},{2,1},{3,2},{4,3},{5,4},{6,5},{7,6},{0,7},{9,8},{10,9},{11,1... | collective-permute-start | bytes 32264 | tf_op jit(solution)/shard_map/ppermute | solution.py:18
  103.5 31.6 %collective-permute-start.8 = (bf16[1,1,64,128]{3,0,2,1:T(2,128)(2,1)}, bf16[1,1,64,128]{3,0,2,1:T(2,128)(2,1)}, u32[]{:S(2)}, u32[]{:S(2)}) collective-permute-start(bf16[1,1,64,128]{3,0,2,1:T(2,128)(2,1)} %slice.156), channel_id=1, source_target_pairs={{0,8},{8,16},{16,24},{24,32},{32,40},{40,48},{48,56},{1,9},{9,17},... | collective-permute-start | bytes 49160 | tf_op jit(solution)/shard_map/ppermute | solution.py:15
  106.8 385.8 %collective-permute-start.9 = (bf16[1,1,64,128]{3,0,2,1:T(2,128)(2,1)}, bf16[1,1,64,128]{3,0,2,1:T(2,128)(2,1)S(1)}, u32[]{:S(2)}, u32[]{:S(2)}) collective-permute-start(bf16[1,1,64,128]{3,0,2,1:T(2,128)(2,1)} %slice.159), channel_id=1, source_target_pairs={{8,0},{16,8},{24,16},{32,24},{40,32},{48,40},{56,48},{9,1},{17,9},... | collective-permute-start | bytes 49160 | tf_op jit(solution)/shard_map/ppermute | solution.py:18
  114.1 16.7 %collective-permute-start.16 = (bf16[1,1,64,128]{3,2,1,0:T(8,128)(2,1)}, bf16[1,1,64,128]{3,2,1,0:T(8,128)(2,1)S(1)}, u32[]{:S(2)}, u32[]{:S(2)}) collective-permute-start(bf16[1,1,64,128]{3,2,1,0:T(8,128)(2,1)} %slice.166), channel_id=1, source_target_pairs={{0,8},{8,16},{16,24},{24,32},{32,40},{40,48},{48,56},{1,9},{9,17},... | collective-permute-start | bytes 49160 | tf_op jit(solution)/shard_map/ppermute | solution.py:15
  117.8 13.1 %collective-permute-start.17 = (bf16[1,1,64,128]{3,1,2,0:T(2,128)(2,1)S(1)}, bf16[1,1,64,128]{3,1,2,0:T(2,128)(2,1)S(1)}, u32[]{:S(2)}, u32[]{:S(2)}) collective-permute-start(bf16[1,1,64,128]{3,1,2,0:T(2,128)(2,1)S(1)} %slice.169), channel_id=1, source_target_pairs={{8,0},{16,8},{24,16},{32,24},{40,32},{48,40},{56,48},{9,1},{17,9},... | collective-permute-start | bytes 49160 | tf_op jit(solution)/shard_map/ppermute | solution.py:18
  490.9 90.9 %reduce-scatter.6.cloned.1.call-start = ((), (), s32[]{:S(2)}) async-start(), calls=%async_computation.4 | async-start | bytes 442368 | tf_op jit(solution)/shard_map/reduce_scatter | solution.py:109
  492.7 30.0 %collective-permute-start.10 = (bf16[1,42,1,128]{3,0,2,1:T(2,128)(2,1)S(1)}, bf16[1,42,1,128]{3,0,2,1:T(2,128)(2,1)}, u32[]{:S(2)}, u32[]{:S(2)}) collective-permute-start(bf16[1,42,1,128]{3,0,2,1:T(2,128)(2,1)S(1)} %get-tuple-element.36), channel_id=1, source_target_pairs={{0,1},{1,2},{2,3},{3,4},{4,5},{5,6},{6,7},{7,0},{8,9},{9,10},{10,1... | collective-permute-start | bytes 32264 | tf_op jit(solution)/shard_map/ppermute | solution.py:15
  492.8 29.9 %collective-permute-start.11 = (bf16[1,42,1,128]{3,0,2,1:T(2,128)(2,1)S(1)}, bf16[1,42,1,128]{3,0,2,1:T(2,128)(2,1)}, u32[]{:S(2)}, u32[]{:S(2)}) collective-permute-start(bf16[1,42,1,128]{3,0,2,1:T(2,128)(2,1)S(1)} %get-tuple-element.37), channel_id=1, source_target_pairs={{1,0},{2,1},{3,2},{4,3},{5,4},{6,5},{7,6},{0,7},{9,8},{10,9},{11,1... | collective-permute-start | bytes 32264 | tf_op jit(solution)/shard_map/ppermute | solution.py:18
  498.3 28.1 %collective-permute-start.20 = (bf16[1,1,64,128]{3,0,2,1:T(2,128)(2,1)S(1)}, bf16[1,1,64,128]{3,0,2,1:T(2,128)(2,1)S(1)}, u32[]{:S(2)}, u32[]{:S(2)}) collective-permute-start(bf16[1,1,64,128]{3,0,2,1:T(2,128)(2,1)S(1)} %slice.172), channel_id=1, source_target_pairs={{0,8},{8,16},{16,24},{24,32},{32,40},{40,48},{48,56},{1,9},{9,17},... | collective-permute-start | bytes 49160 | tf_op jit(solution)/shard_map/ppermute | solution.py:15
  500.2 27.7 %collective-permute-start.21 = (bf16[1,1,64,128]{3,0,2,1:T(2,128)(2,1)S(1)}, bf16[1,1,64,128]{3,0,2,1:T(2,128)(2,1)S(1)}, u32[]{:S(2)}, u32[]{:S(2)}) collective-permute-start(bf16[1,1,64,128]{3,0,2,1:T(2,128)(2,1)S(1)} %slice.175), channel_id=1, source_target_pairs={{8,0},{16,8},{24,16},{32,24},{40,32},{48,40},{56,48},{9,1},{17,9},... | collective-permute-start | bytes 49160 | tf_op jit(solution)/shard_map/ppermute | solution.py:18
  522.6 60.8 %reduce-scatter.4.cloned.1.call-start = ((), (), s32[]{:S(2)}) async-start(), calls=%async_computation.3 | async-start | bytes 442368 | tf_op jit(solution)/shard_map/reduce_scatter | solution.py:106
  528.1 26.3 %collective-permute-start.22 = (bf16[1,42,1,128]{3,0,2,1:T(2,128)(2,1)S(1)}, bf16[1,42,1,128]{3,0,2,1:T(2,128)(2,1)S(1)}, u32[]{:S(2)}, u32[]{:S(2)}) collective-permute-start(bf16[1,42,1,128]{3,0,2,1:T(2,128)(2,1)S(1)} %get-tuple-element.34), channel_id=1, source_target_pairs={{0,1},{1,2},{2,3},{3,4},{4,5},{5,6},{6,7},{7,0},{8,9},{9,10},{10,1... | collective-permute-start | bytes 32264 | tf_op jit(solution)/shard_map/ppermute | solution.py:15
  529.1 25.3 %collective-permute-start.23 = (bf16[1,42,1,128]{3,0,2,1:T(2,128)(2,1)S(1)}, bf16[1,42,1,128]{3,0,2,1:T(2,128)(2,1)S(1)}, u32[]{:S(2)}, u32[]{:S(2)}) collective-permute-start(bf16[1,42,1,128]{3,0,2,1:T(2,128)(2,1)S(1)} %get-tuple-element.35), channel_id=1, source_target_pairs={{1,0},{2,1},{3,2},{4,3},{5,4},{6,5},{7,6},{0,7},{9,8},{10,9},{11,1... | collective-permute-start | bytes 32264 | tf_op jit(solution)/shard_map/ppermute | solution.py:18
  (37 other events, 882.8 us)
Sparse Core Ops, SparseCore 0:
  491.0 25.6 reduce-scatter.7
  522.7 8.5 reduce-scatter.5
  554.5 6.6 reduce-scatter.3
where the time goes:
time: 596 us; the launch traced here: 592 us
  blocking collectives  357 us (60%)
  starting transfers between devices  88.9 us (15%)
  matrix products  59.4 us (10%)
  local copies, waits for them, and re-layouts  41.8 us (7%)
  other arithmetic  29.3 us (5%)
  between operations  14.9 us (2%)
    psum x1, blocking collectives, body(): totals = lax.psum((down_term, mid_term, up_term), ('lat', 'lon'))  347 us
    ppermute x12, starting transfers between devices, extended(): lax.ppermute(lax.slice_in_dim(block, 0, width, axis=dim), axis, backward)  63.1 us
    conv_general_dilated x6, matrix products, convolve(): lax.conv_general_dilated(padded, kernel, (stride, stride), padding, lhs_d...  48.2 us
    ppermute x12, starting transfers between devices, extended(): lax.ppermute(lax.slice_in_dim(block, block.shape[dim] - width, None, axis...  25.5 us
    concatenate x10, other arithmetic, extended(): block = jnp.concatenate([low, block, high], axis=dim)  17 us
    unnamed x76, local copies, waits for them, and re-layouts  16.7 us
    concatenate x22, local copies, waits for them, and re-layouts, extended(): block = jnp.concatenate([low, block, high], axis=dim)  12.3 us
  transfers between devices with their start and end apart: 27, of which 1 were waited for; matrix products, arithmetic and copies ran while one was open for 17% of the time, Pallas kernels for 0%

commit v1 on v0

--- a/solution.py
+++ b/solution.py
@@ -101,7 +101,7 @@
     grad_fields = (
         cotangent.astype(jnp.float32) + taps_up(framed(grad_down_map), swap_io(kernel_down))
     ).astype(jnp.bfloat16)
-    totals = lax.psum((down_term, mid_term, up_term), ("lat", "lon"))
+    totals = lax.psum(lax.psum((down_term, mid_term, up_term), "lon"), "lat")
     grad_down, grad_mid, grad_up = (
         lax.psum_scatter(
             totals[0].astype(jnp.bfloat16), "dp", scatter_dimension=2, tiled=True

time: 596 us -> 392 us (0.66)
  blocking collectives: 357 us -> 99.6 us
  waiting for transfers between devices: 0.98 us -> 64.5 us
  starting transfers between devices: 88.9 us -> 73 us
    psum x1, blocking collectives: 347 us -> 89.8 us  [body(): totals = lax.psum(lax.psum((down_term, mid_term, up_term), 'lon'), 'lat')]
    psum x0 -> x1, waiting for transfers between devices: none -> 62.8 us  [body(): totals = lax.psum(lax.psum((down_term, mid_term, up_term), 'lon'), 'lat')]
    ppermute x12, starting transfers between devices: 63.1 us -> 42.2 us  [extended(): lax.ppermute(lax.slice_in_dim(block, 0, width, axis=dim), axis, backward)]
    unnamed x76 -> x72, local copies, waits for them, and re-layouts: 16.7 us -> 18.5 us
  transfers between devices with their start and end apart: 27 -> 28, of which waited for: 1 -> 2; matrix products, arithmetic and copies ran while one was open for 17% -> 27% of each run, Pallas kernels for 0% -> 0%
where the time goes in v1:
time: 392 us; the launch traced here: 385 us
  blocking collectives  99.6 us (25%)
  starting transfers between devices  73 us (19%)
  waiting for transfers between devices  64.5 us (16%)
  matrix products  61.1 us (16%)
  local copies, waits for them, and re-layouts  44 us (11%)
  other arithmetic  27.8 us (7%)
  between operations  14.9 us (4%)
    psum x1, blocking collectives, body(): totals = lax.psum(lax.psum((down_term, mid_term, up_term), 'lon'), 'lat')  89.8 us
    psum x1, waiting for transfers between devices, body(): totals = lax.psum(lax.psum((down_term, mid_term, up_term), 'lon'), 'lat')  62.8 us
    conv_general_dilated x6, matrix products, convolve(): lax.conv_general_dilated(padded, kernel, (stride, stride), padding, lhs_d...  49.9 us
    ppermute x12, starting transfers between devices, extended(): lax.ppermute(lax.slice_in_dim(block, 0, width, axis=dim), axis, backward)  42.2 us
    ppermute x12, starting transfers between devices, extended(): lax.ppermute(lax.slice_in_dim(block, block.shape[dim] - width, None, axis...  30.7 us
    unnamed x72, local copies, waits for them, and re-layouts  18.5 us
    concatenate x10, other arithmetic, extended(): block = jnp.concatenate([low, block, high], axis=dim)  16.8 us
    concatenate x22, local copies, waits for them, and re-layouts, extended(): block = jnp.concatenate([low, block, high], axis=dim)  13 us
  transfers between devices with their start and end apart: 28, of which 2 were waited for; matrix products, arithmetic and copies ran while one was open for 27% of the time, Pallas kernels for 0%

profile of v1, /device:TPU:16, one launch (start us, length us, event | category | flops | bytes accessed | tf_op | source)
XLA Modules:
  0.0 384.9 jit_solution(6935250728537598364)
XLA Ops:
  10.2 6.1 %collective-permute-start = (bf16[1,1,128,128]{3,2,1,0:T(8,128)(2,1)S(1)}, bf16[1,1,128,128]{3,2,1,0:T(8,128)(2,1)S(1)}, u32[]{:S(2)}, u32[]{:S(2)}) collective-permute-start(bf16[1,1,128,128]{3,2,1,0:T(8,128)(2,1)S(1)} %get-tuple-element.36), channel_id=1, source_target_pairs={{0,8},{8,16},{16,24},{24,32},{32,40},{40,48},{48,56},{1,9},{9,17},... | collective-permute-start | bytes 98312 | tf_op jit(solution)/shard_map/ppermute | solution.py:15
  18.9 6.3 %collective-permute-start.12 = (bf16[1,1,128,128]{3,2,1,0:T(8,128)(2,1)S(1)}, bf16[1,1,128,128]{3,2,1,0:T(8,128)(2,1)S(1)}, u32[]{:S(2)}, u32[]{:S(2)}) collective-permute-start(bf16[1,1,128,128]{3,2,1,0:T(8,128)(2,1)S(1)} %get-tuple-element.34), channel_id=1, source_target_pairs={{0,8},{8,16},{16,24},{24,32},{32,40},{40,48},{48,56},{1,9},{9,17},... | collective-permute-start | bytes 98312 | tf_op jit(solution)/shard_map/ppermute | solution.py:15
  27.6 3.7 all_gather.10
  31.3 3.8 all_gather.11
  42.4 4.6 %collective-permute-start.15 = (bf16[1,82,1,128]{3,2,1,0:T(2,128)(2,1)S(1)}, bf16[1,82,1,128]{3,2,1,0:T(2,128)(2,1)S(1)}, u32[]{:S(2)}, u32[]{:S(2)}) collective-permute-start(bf16[1,82,1,128]{3,2,1,0:T(2,128)(2,1)S(1)} %get-tuple-element.30), channel_id=1, source_target_pairs={{1,0},{2,1},{3,2},{4,3},{5,4},{6,5},{7,6},{0,7},{9,8},{10,9},{11,1... | collective-permute-start | bytes 62984 | tf_op jit(solution)/shard_map/ppermute | solution.py:18
  64.0 5.1 %collective-permute-start.5 = (bf16[1,1,64,128]{3,1,2,0:T(2,128)(2,1)S(1)}, bf16[1,1,64,128]{3,1,2,0:T(2,128)(2,1)S(1)}, u32[]{:S(2)}, u32[]{:S(2)}) collective-permute-start(bf16[1,1,64,128]{3,1,2,0:T(2,128)(2,1)S(1)} %slice.153), channel_id=1, source_target_pairs={{8,0},{16,8},{24,16},{32,24},{40,32},{48,40},{56,48},{9,1},{17,9},... | collective-permute-start | bytes 49160 | tf_op jit(solution)/shard_map/ppermute | solution.py:18
  69.1 4.3 %fusion.132 = (bf16[82,8,18,128,1]{3,1,4,2,0:T(8,128)(2,1)}, bf16[82,1,8,18,128]{4,2,3,0,1:T(8,128)(2,1)S(1)}) fusion(bf16[82,1,7,1,128]{4,2,3,0,1:T(8,128)(2,1)} %get-tuple-element.23, bf16[82,1,8,17,128]{4,2,3,0,1:T(8,128)(2,1)} %slice.186), kind=kLoop, calls=%fused_computation.152 | loop fusion | flops 9068544 | bytes 9047552 | tf_op jit(solution)/shard_map/concatenate | solution.py:19
  80.7 4.1 %collective-permute-start.7 = (bf16[1,42,1,128]{3,1,2,0:T(8,128)(2,1)S(1)}, bf16[1,42,1,128]{3,1,2,0:T(8,128)(2,1)S(1)}, u32[]{:S(2)}, u32[]{:S(2)}) collective-permute-start(bf16[1,42,1,128]{3,1,2,0:T(8,128)(2,1)S(1)} %get-tuple-element.56), channel_id=1, source_target_pairs={{1,0},{2,1},{3,2},{4,3},{5,4},{6,5},{7,6},{0,7},{9,8},{10,9},{11,1... | collective-permute-start | bytes 32264 | tf_op jit(solution)/shard_map/ppermute | solution.py:18
  103.6 3.3 collective-permute-start.8
  106.9 4.6 %collective-permute-start.9 = (bf16[1,1,64,128]{3,0,2,1:T(2,128)(2,1)}, bf16[1,1,64,128]{3,0,2,1:T(2,128)(2,1)S(1)}, u32[]{:S(2)}, u32[]{:S(2)}) collective-permute-start(bf16[1,1,64,128]{3,0,2,1:T(2,128)(2,1)} %slice.159), channel_id=1, source_target_pairs={{8,0},{16,8},{24,16},{32,24},{40,32},{48,40},{56,48},{9,1},{17,9},... | collective-permute-start | bytes 49160 | tf_op jit(solution)/shard_map/ppermute | solution.py:18
  112.2 3.6 collective-permute-start.16
  115.9 4.1 %collective-permute-start.17 = (bf16[1,1,64,128]{3,1,2,0:T(2,128)(2,1)S(1)}, bf16[1,1,64,128]{3,1,2,0:T(2,128)(2,1)S(1)}, u32[]{:S(2)}, u32[]{:S(2)}) collective-permute-start(bf16[1,1,64,128]{3,1,2,0:T(2,128)(2,1)S(1)} %slice.169), channel_id=1, source_target_pairs={{8,0},{16,8},{24,16},{32,24},{40,32},{48,40},{56,48},{9,1},{17,9},... | collective-permute-start | bytes 49160 | tf_op jit(solution)/shard_map/ppermute | solution.py:18
  121.2 5.3 %fusion.79 = f32[3,3,128,128]{3,2,1,0:T(8,128)} fusion(bf16[42,8,9,128,1]{3,1,4,2,0:T(8,128)(2,1)S(1)} %fusion.96, bf16[42,8,9,128,1]{3,1,4,2,0:T(8,128)(2,1)} %get-tuple-element.41, bf16[42,8,9,128,1]{3,1,4,2,0:T(8,128)(2,1)} %copy.67, bf16[40,8,9,128]{3,1,2,0:T(8,128)(2,1)} %copy-done.20, pred[8,9]{0,1:T(8,128)(4,1)S(1)} %copy-done.29), kind=kOutput, calls=%fused_computation.81 | convolution fusion | flops 852185088 | bytes 3649608 | tf_op jit(solution)/shard_map/conv_general_dilated | solution.py:53
  129.0 4.1 %collective-permute-start.19 = (bf16[1,42,1,128]{3,1,2,0:T(8,128)(2,1)S(1)}, bf16[1,42,1,128]{3,1,2,0:T(8,128)(2,1)S(1)}, u32[]{:S(2)}, u32[]{:S(2)}) collective-permute-start(bf16[1,42,1,128]{3,1,2,0:T(8,128)(2,1)S(1)} %get-tuple-element.54), channel_id=1, source_target_pairs={{1,0},{2,1},{3,2},{4,3},{5,4},{6,5},{7,6},{0,7},{9,8},{10,9},{11,1... | collective-permute-start | bytes 32264 | tf_op jit(solution)/shard_map/ppermute | solution.py:18
  138.7 3.6 fusion.76
  145.0 4.2 %collective-permute-start.11 = (bf16[1,42,1,128]{3,0,2,1:T(2,128)(2,1)S(1)}, bf16[1,42,1,128]{3,0,2,1:T(2,128)(2,1)S(1)}, u32[]{:S(2)}, u32[]{:S(2)}) collective-permute-start(bf16[1,42,1,128]{3,0,2,1:T(2,128)(2,1)S(1)} %get-tuple-element.40), channel_id=1, source_target_pairs={{1,0},{2,1},{3,2},{4,3},{5,4},{6,5},{7,6},{0,7},{9,8},{10,9},{11,1... | collective-permute-start | bytes 32264 | tf_op jit(solution)/shard_map/ppermute | solution.py:18
  150.6 4.5 %collective-permute-start.20 = (bf16[1,1,64,128]{3,0,2,1:T(2,128)(2,1)S(1)}, bf16[1,1,64,128]{3,0,2,1:T(2,128)(2,1)S(1)}, u32[]{:S(2)}, u32[]{:S(2)}) collective-permute-start(bf16[1,1,64,128]{3,0,2,1:T(2,128)(2,1)S(1)} %slice.172), channel_id=1, source_target_pairs={{0,8},{8,16},{16,24},{24,32},{32,40},{40,48},{48,56},{1,9},{9,17},... | collective-permute-start | bytes 49160 | tf_op jit(solution)/shard_map/ppermute | solution.py:15
  158.0 3.0 pad_maximum_fusion.15
  162.5 62.8 %all-reduce.5.cloned.1.call-done = (f32[3,3,128,128]{3,2,1,0:T(8,128)}, f32[3,3,128,128]{3,2,1,0:T(8,128)}, f32[3,3,128,128]{3,2,1,0:T(8,128)}) async-done(((f32[3,3,128,128]{3,2,1,0:T(8,128)}, f32[3,3,128,128]{3,2,1,0:T(8,128)}, f32[3,3,128,128]{3,2,1,0:T(8,128)}), (f32[3,3,128,128]{3,2,1,0:T(8,128)}, f32[3,3,128,128]{3,2,1,0:T(8,128)}, f32[3,3,128,128]{3,2,1,0:T(8,128)})) %all-reduce.5.cloned.1.call-update) | async-done | bytes 1769488 | tf_op jit(solution)/shard_map/psum | solution.py:104
  225.3 89.8 %all-reduce.6 = (bf16[3,3,128,128]{3,2,1,0:T(8,128)(2,1)}, bf16[3,3,128,128]{3,2,1,0:T(8,128)(2,1)}, bf16[3,3,128,128]{3,2,1,0:T(8,128)(2,1)}) all-reduce(f32[3,3,128,128]{3,2,1,0:T(8,128)} %get-tuple-element.15, f32[3,3,128,128]{3,2,1,0:T(8,128)} %get-tuple-element.16, ...), channel_id=1, replica_groups=mesh['dp'=2,'lat'=8,'lon'=8] {'lat'}, use_global_device_ids=true, to_apply=%region_1.2 | all-reduce | flops 442368 | bytes 2654208 | tf_op jit(solution)/shard_map/psum | solution.py:104
  315.2 3.6 copy_dynamic-update-slice_fusion
  324.5 20.9 %fusion.21 = bf16[1,80,128,128]{3,0,2,1:T(2,128)(2,1)S(1)} fusion(bf16[1,80,128,128]{3,2,1,0:T(8,128)(2,1)S(1)} %copy-done.12, bf16[3,3,128,128]{3,2,1,0:T(8,128)(2,1)S(1)} %copy-done.27, bf16[1,42,66,128]{3,0,2,1:T(2,128)(2,1)} %pad_maximum_fusion.15), kind=kOutput, calls=%fused_computation.25 | convolution fusion | flops 758906880 | bytes 6247424 | tf_op jit(solution)/shard_map/conv_general_dilated | solution.py:29
  347.4 3.0 pad_maximum_fusion.14
  350.4 20.8 %fusion.19 = bf16[1,80,128,128]{3,0,2,1:T(2,128)(2,1)S(1)} fusion(bf16[1,80,128,128]{3,2,1,0:T(8,128)(2,1)S(1)} %copy-done.14, bf16[3,3,128,128]{3,2,1,0:T(8,128)(2,1)S(1)} %copy-done.25, bf16[1,42,66,128]{3,0,2,1:T(2,128)(2,1)} %pad_maximum_fusion.14), kind=kOutput, calls=%fused_computation.22 | convolution fusion | flops 758906880 | bytes 6247424 | tf_op jit(solution)/shard_map/conv_general_dilated | solution.py:29
  (212 shorter events, 90.7 us)
Async XLA Ops:
  7.2 218.2 %all-reduce.5.cloned.1.call-start = ((), (), s32[]{:S(2)}) async-start(), calls=%async_computation.6 | async-start | bytes 3538944 | tf_op jit(solution)/shard_map/psum | solution.py:104
  8.0 29.5 %collective-permute-start.1 = (bf16[1,1,128,128]{3,2,1,0:T(8,128)(2,1)S(1)}, bf16[1,1,128,128]{3,2,1,0:T(8,128)(2,1)S(1)}, u32[]{:S(2)}, u32[]{:S(2)}) collective-permute-start(bf16[1,1,128,128]{3,2,1,0:T(8,128)(2,1)S(1)} %get-tuple-element.35), channel_id=1, source_target_pairs={{8,0},{16,8},{24,16},{32,24},{40,32},{48,40},{56,48},{9,1},{17,9},... | collective-permute-start | bytes 98312 | tf_op jit(solution)/shard_map/ppermute | solution.py:18
  10.2 25.0 %collective-permute-start = (bf16[1,1,128,128]{3,2,1,0:T(8,128)(2,1)S(1)}, bf16[1,1,128,128]{3,2,1,0:T(8,128)(2,1)S(1)}, u32[]{:S(2)}, u32[]{:S(2)}) collective-permute-start(bf16[1,1,128,128]{3,2,1,0:T(8,128)(2,1)S(1)} %get-tuple-element.36), channel_id=1, source_target_pairs={{0,8},{8,16},{16,24},{24,32},{32,40},{40,48},{48,56},{1,9},{9,17},... | collective-permute-start | bytes 98312 | tf_op jit(solution)/shard_map/ppermute | solution.py:15
  17.0 25.2 %collective-permute-start.13 = (bf16[1,1,128,128]{3,2,1,0:T(8,128)(2,1)S(1)}, bf16[1,1,128,128]{3,2,1,0:T(8,128)(2,1)S(1)}, u32[]{:S(2)}, u32[]{:S(2)}) collective-permute-start(bf16[1,1,128,128]{3,2,1,0:T(8,128)(2,1)S(1)} %get-tuple-element.33), channel_id=1, source_target_pairs={{8,0},{16,8},{24,16},{32,24},{40,32},{48,40},{56,48},{9,1},{17,9},... | collective-permute-start | bytes 98312 | tf_op jit(solution)/shard_map/ppermute | solution.py:18
  18.9 18.7 %collective-permute-start.12 = (bf16[1,1,128,128]{3,2,1,0:T(8,128)(2,1)S(1)}, bf16[1,1,128,128]{3,2,1,0:T(8,128)(2,1)S(1)}, u32[]{:S(2)}, u32[]{:S(2)}) collective-permute-start(bf16[1,1,128,128]{3,2,1,0:T(8,128)(2,1)S(1)} %get-tuple-element.34), channel_id=1, source_target_pairs={{0,8},{8,16},{16,24},{24,32},{32,40},{40,48},{48,56},{1,9},{9,17},... | collective-permute-start | bytes 98312 | tf_op jit(solution)/shard_map/ppermute | solution.py:15
  42.3 11.2 %collective-permute-start.14 = (bf16[1,82,1,128]{3,2,1,0:T(2,128)(2,1)S(1)}, bf16[1,82,1,128]{3,2,1,0:T(2,128)(2,1)S(1)}, u32[]{:S(2)}, u32[]{:S(2)}) collective-permute-start(bf16[1,82,1,128]{3,2,1,0:T(2,128)(2,1)S(1)} %get-tuple-element.29), channel_id=1, source_target_pairs={{0,1},{1,2},{2,3},{3,4},{4,5},{5,6},{6,7},{7,0},{8,9},{9,10},{10,1... | collective-permute-start | bytes 62984 | tf_op jit(solution)/shard_map/ppermute | solution.py:15
  42.4 11.1 %collective-permute-start.15 = (bf16[1,82,1,128]{3,2,1,0:T(2,128)(2,1)S(1)}, bf16[1,82,1,128]{3,2,1,0:T(2,128)(2,1)S(1)}, u32[]{:S(2)}, u32[]{:S(2)}) collective-permute-start(bf16[1,82,1,128]{3,2,1,0:T(2,128)(2,1)S(1)} %get-tuple-element.30), channel_id=1, source_target_pairs={{1,0},{2,1},{3,2},{4,3},{5,4},{6,5},{7,6},{0,7},{9,8},{10,9},{11,1... | collective-permute-start | bytes 62984 | tf_op jit(solution)/shard_map/ppermute | solution.py:18
  61.5 18.2 %collective-permute-start.4 = (bf16[1,1,64,128]{3,2,1,0:T(8,128)(2,1)S(1)}, bf16[1,1,64,128]{3,2,1,0:T(8,128)(2,1)S(1)}, u32[]{:S(2)}, u32[]{:S(2)}) collective-permute-start(bf16[1,1,64,128]{3,2,1,0:T(8,128)(2,1)S(1)} %slice.150), channel_id=1, source_target_pairs={{0,8},{8,16},{16,24},{24,32},{32,40},{40,48},{48,56},{1,9},{9,17},... | collective-permute-start | bytes 49160 | tf_op jit(solution)/shard_map/ppermute | solution.py:15
  64.0 15.8 %collective-permute-start.5 = (bf16[1,1,64,128]{3,1,2,0:T(2,128)(2,1)S(1)}, bf16[1,1,64,128]{3,1,2,0:T(2,128)(2,1)S(1)}, u32[]{:S(2)}, u32[]{:S(2)}) collective-permute-start(bf16[1,1,64,128]{3,1,2,0:T(2,128)(2,1)S(1)} %slice.153), channel_id=1, source_target_pairs={{8,0},{16,8},{24,16},{32,24},{40,32},{48,40},{56,48},{9,1},{17,9},... | collective-permute-start | bytes 49160 | tf_op jit(solution)/shard_map/ppermute | solution.py:18
  80.6 10.5 %collective-permute-start.6 = (bf16[1,42,1,128]{3,1,2,0:T(8,128)(2,1)S(1)}, bf16[1,42,1,128]{3,1,2,0:T(8,128)(2,1)S(1)}, u32[]{:S(2)}, u32[]{:S(2)}) collective-permute-start(bf16[1,42,1,128]{3,1,2,0:T(8,128)(2,1)S(1)} %get-tuple-element.55), channel_id=1, source_target_pairs={{0,1},{1,2},{2,3},{3,4},{4,5},{5,6},{6,7},{7,0},{8,9},{9,10},{10,1... | collective-permute-start | bytes 32264 | tf_op jit(solution)/shard_map/ppermute | solution.py:15
  80.7 10.5 %collective-permute-start.7 = (bf16[1,42,1,128]{3,1,2,0:T(8,128)(2,1)S(1)}, bf16[1,42,1,128]{3,1,2,0:T(8,128)(2,1)S(1)}, u32[]{:S(2)}, u32[]{:S(2)}) collective-permute-start(bf16[1,42,1,128]{3,1,2,0:T(8,128)(2,1)S(1)} %get-tuple-element.56), channel_id=1, source_target_pairs={{1,0},{2,1},{3,2},{4,3},{5,4},{6,5},{7,6},{0,7},{9,8},{10,9},{11,1... | collective-permute-start | bytes 32264 | tf_op jit(solution)/shard_map/ppermute | solution.py:18
  103.6 38.8 %collective-permute-start.8 = (bf16[1,1,64,128]{3,0,2,1:T(2,128)(2,1)}, bf16[1,1,64,128]{3,0,2,1:T(2,128)(2,1)}, u32[]{:S(2)}, u32[]{:S(2)}) collective-permute-start(bf16[1,1,64,128]{3,0,2,1:T(2,128)(2,1)} %slice.156), channel_id=1, source_target_pairs={{0,8},{8,16},{16,24},{24,32},{32,40},{40,48},{48,56},{1,9},{9,17},... | collective-permute-start | bytes 49160 | tf_op jit(solution)/shard_map/ppermute | solution.py:15
  106.9 37.8 %collective-permute-start.9 = (bf16[1,1,64,128]{3,0,2,1:T(2,128)(2,1)}, bf16[1,1,64,128]{3,0,2,1:T(2,128)(2,1)S(1)}, u32[]{:S(2)}, u32[]{:S(2)}) collective-permute-start(bf16[1,1,64,128]{3,0,2,1:T(2,128)(2,1)} %slice.159), channel_id=1, source_target_pairs={{8,0},{16,8},{24,16},{32,24},{40,32},{48,40},{56,48},{9,1},{17,9},... | collective-permute-start | bytes 49160 | tf_op jit(solution)/shard_map/ppermute | solution.py:18
  112.2 16.7 %collective-permute-start.16 = (bf16[1,1,64,128]{3,2,1,0:T(8,128)(2,1)}, bf16[1,1,64,128]{3,2,1,0:T(8,128)(2,1)S(1)}, u32[]{:S(2)}, u32[]{:S(2)}) collective-permute-start(bf16[1,1,64,128]{3,2,1,0:T(8,128)(2,1)} %slice.166), channel_id=1, source_target_pairs={{0,8},{8,16},{16,24},{24,32},{32,40},{40,48},{48,56},{1,9},{9,17},... | collective-permute-start | bytes 49160 | tf_op jit(solution)/shard_map/ppermute | solution.py:15
  115.9 13.1 %collective-permute-start.17 = (bf16[1,1,64,128]{3,1,2,0:T(2,128)(2,1)S(1)}, bf16[1,1,64,128]{3,1,2,0:T(2,128)(2,1)S(1)}, u32[]{:S(2)}, u32[]{:S(2)}) collective-permute-start(bf16[1,1,64,128]{3,1,2,0:T(2,128)(2,1)S(1)} %slice.169), channel_id=1, source_target_pairs={{8,0},{16,8},{24,16},{32,24},{40,32},{48,40},{56,48},{9,1},{17,9},... | collective-permute-start | bytes 49160 | tf_op jit(solution)/shard_map/ppermute | solution.py:18
  142.4 230.9 %reduce-scatter.8.cloned.1.call-start = ((), (), s32[]{:S(2)}) async-start(), calls=%async_computation.5 | async-start | bytes 442368 | tf_op jit(solution)/shard_map/reduce_scatter | solution.py:112
  144.8 13.2 %collective-permute-start.10 = (bf16[1,42,1,128]{3,0,2,1:T(2,128)(2,1)S(1)}, bf16[1,42,1,128]{3,0,2,1:T(2,128)(2,1)S(1)}, u32[]{:S(2)}, u32[]{:S(2)}) collective-permute-start(bf16[1,42,1,128]{3,0,2,1:T(2,128)(2,1)S(1)} %get-tuple-element.39), channel_id=1, source_target_pairs={{0,1},{1,2},{2,3},{3,4},{4,5},{5,6},{6,7},{7,0},{8,9},{9,10},{10,1... | collective-permute-start | bytes 32264 | tf_op jit(solution)/shard_map/ppermute | solution.py:15
  145.0 13.0 %collective-permute-start.11 = (bf16[1,42,1,128]{3,0,2,1:T(2,128)(2,1)S(1)}, bf16[1,42,1,128]{3,0,2,1:T(2,128)(2,1)S(1)}, u32[]{:S(2)}, u32[]{:S(2)}) collective-permute-start(bf16[1,42,1,128]{3,0,2,1:T(2,128)(2,1)S(1)} %get-tuple-element.40), channel_id=1, source_target_pairs={{1,0},{2,1},{3,2},{4,3},{5,4},{6,5},{7,6},{0,7},{9,8},{10,9},{11,1... | collective-permute-start | bytes 32264 | tf_op jit(solution)/shard_map/ppermute | solution.py:18
  150.6 11.3 %collective-permute-start.20 = (bf16[1,1,64,128]{3,0,2,1:T(2,128)(2,1)S(1)}, bf16[1,1,64,128]{3,0,2,1:T(2,128)(2,1)S(1)}, u32[]{:S(2)}, u32[]{:S(2)}) collective-permute-start(bf16[1,1,64,128]{3,0,2,1:T(2,128)(2,1)S(1)} %slice.172), channel_id=1, source_target_pairs={{0,8},{8,16},{16,24},{24,32},{32,40},{40,48},{48,56},{1,9},{9,17},... | collective-permute-start | bytes 49160 | tf_op jit(solution)/shard_map/ppermute | solution.py:15
  155.1 163.6 %collective-permute-start.21 = (bf16[1,1,64,128]{3,0,2,1:T(2,128)(2,1)S(1)}, bf16[1,1,64,128]{3,0,2,1:T(2,128)(2,1)S(1)}, u32[]{:S(2)}, u32[]{:S(2)}) collective-permute-start(bf16[1,1,64,128]{3,0,2,1:T(2,128)(2,1)S(1)} %slice.175), channel_id=1, source_target_pairs={{8,0},{16,8},{24,16},{32,24},{40,32},{48,40},{56,48},{9,1},{17,9},... | collective-permute-start | bytes 49160 | tf_op jit(solution)/shard_map/ppermute | solution.py:18
  315.1 59.8 %reduce-scatter.6.cloned.1.call-start = ((), (), s32[]{:S(2)}) async-start(), calls=%async_computation.4 | async-start | bytes 442368 | tf_op jit(solution)/shard_map/reduce_scatter | solution.py:109
  320.2 27.2 %collective-permute-start.22 = (bf16[1,42,1,128]{3,0,2,1:T(2,128)(2,1)S(1)}, bf16[1,42,1,128]{3,0,2,1:T(2,128)(2,1)S(1)}, u32[]{:S(2)}, u32[]{:S(2)}) collective-permute-start(bf16[1,42,1,128]{3,0,2,1:T(2,128)(2,1)S(1)} %get-tuple-element.37), channel_id=1, source_target_pairs={{0,1},{1,2},{2,3},{3,4},{4,5},{5,6},{6,7},{7,0},{8,9},{9,10},{10,1... | collective-permute-start | bytes 32264 | tf_op jit(solution)/shard_map/ppermute | solution.py:15
  322.7 24.7 %collective-permute-start.23 = (bf16[1,42,1,128]{3,0,2,1:T(2,128)(2,1)S(1)}, bf16[1,42,1,128]{3,0,2,1:T(2,128)(2,1)S(1)}, u32[]{:S(2)}, u32[]{:S(2)}) collective-permute-start(bf16[1,42,1,128]{3,0,2,1:T(2,128)(2,1)S(1)} %get-tuple-element.38), channel_id=1, source_target_pairs={{1,0},{2,1},{3,2},{4,3},{5,4},{6,5},{7,6},{0,7},{9,8},{10,9},{11,1... | collective-permute-start | bytes 32264 | tf_op jit(solution)/shard_map/ppermute | solution.py:18
  324.4 52.2 %reduce-scatter.4.cloned.1.call-start = ((), (), s32[]{:S(2)}) async-start(), calls=%async_computation.3 | async-start | bytes 442368 | tf_op jit(solution)/shard_map/reduce_scatter | solution.py:106
  (36 other events, 475.0 us)
Sparse Core Ops, SparseCore 0:
  142.5 82.7 all-reduce.4
  315.2 11.4 reduce-scatter.7
  329.7 11.7 reduce-scatter.5
  350.5 9.7 reduce-scatter.3
